TPU v7x, 32 devices: a whole 2x2x4 slice. The times are simulated.
32 devices in a mesh: pair: 8 (over z, x), pw: 4 (over y, core).
Axes of the slice: x: 2, y: 2, z: 4, core: 2. Of those that a mesh axis runs over, the one named last changes fastest.
Arguments:
- pair_matrix: bfloat16 [384, 12288], P('pair', 'pw'), may hold values from -6 to 6
- basis: bfloat16 [12288, 768], P('pw'), may hold values from -0.078125 to 0.078125
- valence: int32 [384], P('pair'), may hold values from 0 to 127
- conduction: int32 [384], P('pair'), may hold values from 64 to 255
- occupation: int32 [256], replicated, may hold values from 0 to 2
- energy: int32 [256], replicated, may hold values from 0 to 999
Outputs:
- chi: float32 [2, 768, 768], P(None, 'pair', 'pw')
All inputs are finite; a program needn't handle non-finite values.
Results may differ from a plain program's by a relative error of at most 0.005.
Values may be sent and summed in bfloat16 or wider, within the bound.
No kernel may reach another device: no remote copies, remote signals or barrier semaphores. Data moves between devices by JAX's collectives and lax.ppermute only.
A program may use at most 64 MiB of HBM per device.

v0:
```python
import jax
import jax.numpy as jnp
from jax import lax
from jax.sharding import PartitionSpec as P

W = 2


def lookup(index, table):
    bands = table.shape[0]
    match = index[:, None] == jnp.arange(bands)[None, :]
    return jnp.sum(jnp.where(match, table[None, :], 0), axis=1)


def shards(pair_matrix, basis, valence, conduction, occupation, energy):
    pair_count = pair_matrix.shape[0]
    pairs_all = pair_count * lax.axis_size("pair")
    gap = (lookup(conduction, energy) - lookup(valence, energy)).astype(jnp.float32) * 0.01
    filling = (lookup(valence, occupation) - lookup(conduction, occupation)).astype(jnp.float32)
    freq = 0.5 * (jnp.arange(W).astype(jnp.float32) + 1.0)
    weights = filling[None, :] * 2.0 * gap[None, :] / (freq[:, None] ** 2 + gap[None, :] ** 2)
    weights = weights / jnp.sqrt(jnp.float32(pairs_all))
    partial_proj = jnp.dot(pair_matrix, basis, preferred_element_type=jnp.float32)
    owned = lax.psum_scatter(partial_proj, "pw", scatter_dimension=1, tiled=True).astype(
        jnp.bfloat16
    )
    scaled_piece = (
        weights[:, :, None]
        * lax.all_gather(owned, "pw", axis=1, tiled=True).astype(jnp.float32)[None]
    ).astype(jnp.bfloat16)
    term = jnp.einsum("kpa,pb->kab", scaled_piece, owned, preferred_element_type=jnp.float32)
    chi = lax.psum_scatter(term, "pair", scatter_dimension=1, tiled=True)
    return chi


def solution(mesh):
    return jax.shard_map(
        shards,
        mesh=mesh,
        in_specs=(P("pair", "pw"), P("pw", None), P("pair"), P("pair"), P(), P()),
        out_specs=P(None, "pair", "pw"),
        check_vma=False,
    )
```

profile of v0, /device:TPU:0, one launch (start us, length us, event | category | flops | bytes accessed | tf_op | source)
XLA Modules:
  0.0 117.0 jit_solution(15974078954626075413)
XLA Ops:
  6.5 0.0 copy-start
  6.5 0.0 copy-start.1
  6.5 0.0 copy-start.2
  6.5 0.0 copy-start.4
  6.5 0.0 copy-start.3
  6.5 0.0 reduce-scatter.7.cloned.1.call-start
  6.6 0.9 copy-done
  7.5 5.0 %convolution_bitcast_fusion = f32[768,48]{1,0:T(8,128)} fusion(bf16[48,3072]{1,0:T(8,128)(2,1)S(1)} %copy-done, bf16[3072,768]{1,0:T(8,128)(2,1)} %param.7), kind=kOutput, calls=%fused_computation | convolution fusion | flops 226492416 | bytes 5160960
  12.5 0.0 reduce-scatter.7.cloned.1.call-update
  12.5 0.0 reduce-scatter.5.cloned.1.call-start
  12.6 0.0 copy-done.1
  12.6 0.0 copy-done.2
  12.6 0.0 copy-done.4
  12.6 0.0 copy-done.3
  12.6 0.2 select_reduce_fusion
  12.9 0.1 divide_multiply_fusion
  12.9 23.3 %reduce-scatter.7.cloned.1.call-done = f32[192,48]{1,0:T(8,128)} async-done(((f32[768,48]{1,0:T(8,128)}), f32[192,48]{1,0:T(8,128)}) %reduce-scatter.7.cloned.1.call-update) | async-done | bytes 36880
  36.2 1.0 copy.11
  37.2 5.3 %all-gather = bf16[4,192,48]{1,2,0:T(8,128)(2,1)S(1)} all-gather(bf16[1,192,48]{1,2,0:T(8,128)(2,1)S(1)} %bitcast.17), channel_id=1, replica_groups=mesh['pair'=8,'pw'=4] {'pw'}, dimensions={0}, use_global_device_ids=true | all-gather | bytes 92160 | tf_op jit(solution)/shard_map/all_gather | solution.py:29
  42.6 0.1 copy.9
  42.6 0.1 reshape.79
  42.8 1.6 %fusion = f32[2,768,192]{2,1,0:T(8,128)} fusion(f32[48,768]{1,0:T(8,128)S(1)} %bitcast.16, f32[2,48]{1,0:T(2,128)S(1)} %divide_multiply_fusion, bf16[48,192]{1,0:T(8,128)(2,1)S(1)} %copy.11), kind=kOutput, calls=%fused_computation.2 | convolution fusion | flops 28459008 | bytes 1345920 | tf_op jit(solution)/shard_map/kpa,pb->kab/dot_general | solution.py:31
  44.4 0.0 reduce-scatter.5.cloned.1.call-update
  44.4 65.7 %reduce-scatter.5.cloned.1.call-done = f32[2,96,192]{2,1,0:T(8,128)} async-done(((f32[2,768,192]{2,1,0:T(8,128)}), f32[2,96,192]{2,1,0:T(8,128)}) %reduce-scatter.5.cloned.1.call-update) | async-done | bytes 147472 | tf_op jit(solution)/shard_map/reduce_scatter | solution.py:32
  (2 shorter events, 0.0 us)
Async XLA Ops:
  6.5 1.0 copy-start
  6.5 6.0 %copy-start.1 = (s32[256]{0:T(256)S(1)}, s32[256]{0:T(256)}, u32[]{:S(2)}) copy-start(s32[256]{0:T(256)} %param.11) | copy-start | bytes 3076
  6.5 6.1 %copy-start.2 = (s32[256]{0:T(256)S(1)}, s32[256]{0:T(256)}, u32[]{:S(2)}) copy-start(s32[256]{0:T(256)} %param.10) | copy-start | bytes 3076
  6.5 6.1 %copy-start.4 = (s32[48]{0:T(128)S(1)}, s32[48]{0:T(128)}, u32[]{:S(2)}) copy-start(s32[48]{0:T(128)} %param.9) | copy-start | bytes 580
  6.5 6.1 %copy-start.3 = (s32[48]{0:T(128)S(1)}, s32[48]{0:T(128)}, u32[]{:S(2)}) copy-start(s32[48]{0:T(128)} %param.8) | copy-start | bytes 580
  6.5 29.7 %reduce-scatter.7.cloned.1.call-start = ((), (), s32[]{:S(2)}) async-start(), calls=%async_computation.3 | async-start | bytes 491520
  12.5 97.6 %reduce-scatter.5.cloned.1.call-start = ((), (), s32[]{:S(2)}) async-start(), calls=%async_computation.2 | async-start | bytes 1769472 | tf_op jit(solution)/shard_map/reduce_scatter | solution.py:32
Sparse Core Ops, SparseCore 0:
  12.7 23.5 reduce-scatter.6
  44.5 65.5 reduce-scatter.4
where the time goes:
time: 117 us
  waiting for transfers between devices  89.1 us (76%)
  between operations  13.5 us (12%)
  matrix products  6.65 us (6%)
  blocking collectives  5.33 us (5%)
  local copies, waits for them, and re-layouts  2.08 us (2%)
    reduce_scatter x1, waiting for transfers between devices, shards(): chi = lax.psum_scatter(term, 'pair', scatter_dimension=1, tiled=True)  65.7 us
    unnamed x3, waiting for transfers between devices  23.3 us
    all_gather x1, blocking collectives, shards(): lax.all_gather(owned, 'pw', axis=1, tiled=True).astype(jnp.float32)[None]  5.33 us
    unnamed x1, matrix products  5.01 us
  transfers between devices with their start and end apart: 2, of which 2 were waited for; matrix products, arithmetic and copies ran while one was open for 0% of the time, Pallas kernels for 0%

commit v1 on v0

v1 whole, which is shorter than its diff:
```python
import jax
import jax.numpy as jnp
from jax import lax
from jax.sharding import PartitionSpec as P

W = 2


def lookup(index, table):
    bands = table.shape[0]
    match = index[:, None] == jnp.arange(bands)[None, :]
    return jnp.sum(jnp.where(match, table[None, :], 0), axis=1)


def three_parts(w):
    parts = []
    for _ in range(3):
        top = lax.reduce_precision(w, 8, 7)
        parts.append(top.astype(jnp.bfloat16))
        w = w - top
    return parts


def shards(pair_matrix, basis, valence, conduction, occupation, energy):
    rows = pair_matrix.shape[0]
    modes = basis.shape[1]
    n_pair, n_pw = lax.axis_size("pair"), lax.axis_size("pw")
    a_cols, b_cols, half = modes // n_pair, modes // n_pw, modes // 2
    me_pw = lax.axis_index("pw")

    gap = (lookup(conduction, energy) - lookup(valence, energy)).astype(jnp.float32) * 0.01
    filling = (lookup(valence, occupation) - lookup(conduction, occupation)).astype(jnp.float32)
    freq = 0.5 * (jnp.arange(W).astype(jnp.float32) + 1.0)
    weights = filling[None, :] * 2.0 * gap[None, :] / (freq[:, None] ** 2 + gap[None, :] ** 2)
    weights = weights / jnp.sqrt(jnp.float32(rows * n_pair))
    weight_cols = jnp.stack(three_parts(weights), 0).reshape(3 * W, rows).T

    def swap(x, bit):
        return lax.ppermute(x, "pw", [(j, j ^ bit) for j in range(n_pw)])

    partial = jnp.dot(pair_matrix, basis, preferred_element_type=jnp.float32)
    low, high = partial[:, :half], partial[:, half:]
    odd = me_pw % 2 == 1
    mine = jnp.where(odd, high, low)
    mine = mine + swap(jnp.where(odd, low, high), 1)
    bit = 2
    while bit < n_pw:
        mine = mine + swap(mine, bit)
        bit *= 2
    mine = mine.astype(jnp.bfloat16)
    other = swap(mine, 1)
    proj = jnp.concatenate([jnp.where(odd, other, mine), jnp.where(odd, mine, other)], axis=1)

    left = proj.reshape(rows, n_pair, a_cols).transpose(1, 0, 2)
    right = lax.dynamic_slice_in_dim(proj, me_pw * b_cols, b_cols, axis=1)
    tail = jnp.concatenate([right, weight_cols], axis=1)
    message = jnp.concatenate(
        [left, jnp.broadcast_to(tail[None], (n_pair,) + tail.shape)], axis=2
    )
    message = lax.all_to_all(message, "pair", 0, 0, tiled=True).reshape(n_pair * rows, -1)

    left, right = message[:, :a_cols], message[:, a_cols : a_cols + b_cols]
    w = message[:, a_cols + b_cols :].astype(jnp.float32).reshape(-1, 3, W).sum(axis=1)
    scaled = (w[:, :, None] * left.astype(jnp.float32)[:, None, :]).astype(jnp.bfloat16)
    return jnp.einsum("pka,pb->kab", scaled, right, preferred_element_type=jnp.float32)


def solution(mesh):
    return jax.shard_map(
        shards,
        mesh=mesh,
        in_specs=(P("pair", "pw"), P("pw", None), P("pair"), P("pair"), P(), P()),
        out_specs=P(None, "pair", "pw"),
        check_vma=False,
    )
```

time: 117 us -> 31.2 us (0.27)
  waiting for transfers between devices: 89.1 us -> 4.22 us
  between operations: 13.5 us -> 0.16 us
  blocking collectives: 5.33 us -> 16.5 us
  starting transfers between devices: 0.08 us -> 3.55 us
  matrix products: 6.65 us -> 4.18 us
    reduce_scatter x1 -> x0, waiting for transfers between devices: 65.7 us -> none  [shards(): chi = lax.psum_scatter(term, 'pair', scatter_dimension=1, tiled=True)]
    unnamed x3 -> x0, waiting for transfers between devices: 23.3 us -> none
    all_to_all x0 -> x1, blocking collectives: none -> 16.5 us  [shards(): lax.all_to_all(message, 'pair', 0, 0, tiled=True).reshape(n_pair * rows, -1)]
    all_gather x1 -> x0, blocking collectives: 5.33 us -> none  [shards(): lax.all_gather(owned, 'pw', axis=1, tiled=True).astype(jnp.float32)[None]]
    unnamed x1 -> x0, matrix products: 5.01 us -> none
    ppermute x0 -> x3, waiting for transfers between devices: none -> 4.22 us  [swap(): return lax.ppermute(x, 'pw', [(j, j ^ bit) for j in range(n_pw)])]
    ppermute x0 -> x3, starting transfers between devices: none -> 3.55 us  [swap(): return lax.ppermute(x, 'pw', [(j, j ^ bit) for j in range(n_pw)])]
    dot_general x1 -> x2, matrix products: 1.63 us -> 4.18 us  [the longest x1 3.2 us: shards(): partial = jnp.dot(pair_matrix, basis, preferred_element_type=jnp.float32)]
  transfers between devices with their start and end apart: 2 -> 3, of which waited for: 2 -> 3; matrix products, arithmetic and copies ran while one was open for 0% -> 1% of each run, Pallas kernels for 0% -> 0%
where the time goes in v1:
time: 31.2 us; the launch traced here: 31 us
  blocking collectives  16.5 us (53%)
  waiting for transfers between devices  4.22 us (14%)
  matrix products  4.18 us (13%)
  starting transfers between devices  3.55 us (11%)
  local copies, waits for them, and re-layouts  1.57 us (5%)
  other arithmetic  0.76 us (2%)
    all_to_all x1, blocking collectives, shards(): lax.all_to_all(message, 'pair', 0, 0, tiled=True).reshape(n_pair * rows, -1)  16.5 us
    ppermute x3, waiting for transfers between devices, swap(): return lax.ppermute(x, 'pw', [(j, j ^ bit) for j in range(n_pw)])  4.22 us
    ppermute x3, starting transfers between devices, swap(): return lax.ppermute(x, 'pw', [(j, j ^ bit) for j in range(n_pw)])  3.55 us
    dot_general x1, matrix products, shards(): partial = jnp.dot(pair_matrix, basis, preferred_element_type=jnp.float32)  3.2 us
    unnamed x12, local copies, waits for them, and re-layouts  1.14 us
    dot_general x1, matrix products, shards(): jnp.einsum('pka,pb->kab', scaled, right, preferred_element_type=jnp.float32)  0.98 us
  transfers between devices with their start and end apart: 3, of which 3 were waited for; matrix products, arithmetic and copies ran while one was open for 1% of the time, Pallas kernels for 0%

profile of v1, /device:TPU:0, one launch (start us, length us, event | category | flops | bytes accessed | tf_op | source)
XLA Modules:
  0.0 31.0 jit_solution(12654697657567786882)
XLA Ops:
  0.0 0.0 copy-start
  0.0 0.0 copy-start.1
  0.0 0.0 copy-start.2
  0.0 0.0 copy-start.4
  0.0 0.0 copy-start.3
  0.0 0.9 %copy-done = bf16[48,3072]{1,0:T(8,128)(2,1)S(1)} copy-done((bf16[48,3072]{1,0:T(8,128)(2,1)S(1)}, bf16[48,3072]{1,0:T(8,128)(2,1)}, u32[]{:S(2)}) %copy-start) | copy-done | bytes 294936
  1.0 3.2 %fusion.7 = f32[48,768]{1,0:T(8,128)S(1)} fusion(bf16[48,3072]{1,0:T(8,128)(2,1)S(1)} %copy-done, bf16[3072,768]{1,0:T(8,128)(2,1)} %param.7), kind=kOutput, calls=%fused_computation.35 | convolution fusion | flops 226492416 | bytes 5160960 | tf_op jit(solution)/shard_map/dot_general | solution.py:41
  4.2 0.6 %collective-permute-start = (f32[48,384]{1,0:T(8,128)S(1)}, f32[48,384]{1,0:T(8,128)S(1)}, u32[]{:S(2)}, u32[]{:S(2)}) collective-permute-start(f32[48,384]{1,0:T(8,128)S(1)} %slice_select_fusion), channel_id=1, source_target_pairs={{0,1},{1,0},{2,3},{3,2},{4,5},{5,4},{6,7},{7,6},{8,9},{9,8},{10,11... | collective-permute-start | bytes 221192 | tf_op jit(solution)/shard_map/ppermute | solution.py:39
  4.7 0.0 copy-done.1
  4.8 0.0 copy-done.2
  4.8 0.0 copy-done.4
  4.8 0.0 copy-done.3
  4.8 0.2 select_reduce_fusion
  5.0 0.7 %collective-permute-done = f32[48,384]{1,0:T(8,128)S(1)} collective-permute-done((f32[48,384]{1,0:T(8,128)S(1)}, f32[48,384]{1,0:T(8,128)S(1)}, u32[]{:S(2)}, u32[]{:S(2)}) %collective-permute-start) | collective-permute-done | bytes 73760 | tf_op jit(solution)/shard_map/ppermute | solution.py:39
  5.7 2.9 %collective-permute-start.1 = (f32[48,384]{1,0:T(8,128)S(1)}, f32[48,384]{1,0:T(8,128)S(1)}, u32[]{:S(2)}, u32[]{:S(2)}) collective-permute-start(f32[48,384]{1,0:T(8,128)S(1)} %select_add_fusion), channel_id=1, source_target_pairs={{0,2},{1,3},{2,0},{3,1},{4,6},{5,7},{6,4},{7,5},{8,10},{9,11},{10,... | collective-permute-start | bytes 221192 | tf_op jit(solution)/shard_map/ppermute | solution.py:39
  8.6 0.1 reduce-precision_convert_fusion.1
  8.7 2.5 %collective-permute-done.1 = f32[48,384]{1,0:T(8,128)S(1)} collective-permute-done((f32[48,384]{1,0:T(8,128)S(1)}, f32[48,384]{1,0:T(8,128)S(1)}, u32[]{:S(2)}, u32[]{:S(2)}) %collective-permute-start.1) | collective-permute-done | bytes 73760 | tf_op jit(solution)/shard_map/ppermute | solution.py:39
  11.2 0.1 collective-permute-start.2
  11.3 0.1 copy.24
  11.4 1.1 %collective-permute-done.2 = bf16[48,384]{1,0:T(8,128)(2,1)S(1)} collective-permute-done((bf16[48,384]{1,0:T(8,128)(2,1)S(1)}, bf16[48,384]{1,0:T(8,128)(2,1)S(1)}, u32[]{:S(2)}, u32[]{:S(2)}) %collective-permute-start.2) | collective-permute-done | bytes 36896 | tf_op jit(solution)/shard_map/ppermute | solution.py:39
  12.5 0.1 fusion.3
  12.6 0.1 reshape.269
  12.8 0.1 pad_maximum_fusion.2
  12.9 0.1 pad_maximum_fusion
  13.1 16.5 %all_to_all.5 = bf16[8,48,294]{2,1,0:T(8,128)(2,1)S(1)} all-to-all(bf16[8,48,294]{2,1,0:T(8,128)(2,1)S(1)} %pad_maximum_fusion), channel_id=1, replica_groups=mesh['pair'=8,'pw'=4] {'pair'}, dimensions={0} | all-to-all | bytes 451584 | tf_op jit(solution)/shard_map/all_to_all | solution.py:60
  29.6 0.1 slice.22
  29.7 0.1 copy.29
  29.8 0.1 copy.28
  30.0 1.0 %fusion = f32[2,96,192]{2,1,0:T(8,128)} fusion(bf16[384,294]{1,0:T(8,128)(2,1)S(1)} %bitcast.15, f32[384,96]{0,1:T(8,128)S(1)} %convert_element_type.71, f32[384,2]{0,1:T(2,128)S(1)} %reduce_sum.49), kind=kOutput, calls=%fused_computation.3 | convolution fusion | flops 28459008 | bytes 494592 | tf_op jit(solution)/shard_map/pka,pb->kab/dot_general | solution.py:65
  (15 shorter events, 0.2 us)
Async XLA Ops:
  0.0 1.0 %copy-start = (bf16[48,3072]{1,0:T(8,128)(2,1)S(1)}, bf16[48,3072]{1,0:T(8,128)(2,1)}, u32[]{:S(2)}) copy-start(bf16[48,3072]{1,0:T(8,128)(2,1)} %param.6) | copy-start | bytes 884740
  0.0 4.7 %copy-start.1 = (s32[256]{0:T(256)S(1)}, s32[256]{0:T(256)}, u32[]{:S(2)}) copy-start(s32[256]{0:T(256)} %param.11) | copy-start | bytes 3076
  0.0 4.7 %copy-start.2 = (s32[256]{0:T(256)S(1)}, s32[256]{0:T(256)}, u32[]{:S(2)}) copy-start(s32[256]{0:T(256)} %param.10) | copy-start | bytes 3076
  0.0 4.7 %copy-start.4 = (s32[48]{0:T(128)S(1)}, s32[48]{0:T(128)}, u32[]{:S(2)}) copy-start(s32[48]{0:T(128)} %param.9) | copy-start | bytes 580
  0.0 4.7 %copy-start.3 = (s32[48]{0:T(128)S(1)}, s32[48]{0:T(128)}, u32[]{:S(2)}) copy-start(s32[48]{0:T(128)} %param.8) | copy-start | bytes 580
  4.2 1.5 %collective-permute-start = (f32[48,384]{1,0:T(8,128)S(1)}, f32[48,384]{1,0:T(8,128)S(1)}, u32[]{:S(2)}, u32[]{:S(2)}) collective-permute-start(f32[48,384]{1,0:T(8,128)S(1)} %slice_select_fusion), channel_id=1, source_target_pairs={{0,1},{1,0},{2,3},{3,2},{4,5},{5,4},{6,7},{7,6},{8,9},{9,8},{10,11... | collective-permute-start | bytes 221192 | tf_op jit(solution)/shard_map/ppermute | solution.py:39
  5.7 5.5 %collective-permute-start.1 = (f32[48,384]{1,0:T(8,128)S(1)}, f32[48,384]{1,0:T(8,128)S(1)}, u32[]{:S(2)}, u32[]{:S(2)}) collective-permute-start(f32[48,384]{1,0:T(8,128)S(1)} %select_add_fusion), channel_id=1, source_target_pairs={{0,2},{1,3},{2,0},{3,1},{4,6},{5,7},{6,4},{7,5},{8,10},{9,11},{10,... | collective-permute-start | bytes 221192 | tf_op jit(solution)/shard_map/ppermute | solution.py:39
  11.2 1.3 %collective-permute-start.2 = (bf16[48,384]{1,0:T(8,128)(2,1)S(1)}, bf16[48,384]{1,0:T(8,128)(2,1)S(1)}, u32[]{:S(2)}, u32[]{:S(2)}) collective-permute-start(bf16[48,384]{1,0:T(8,128)(2,1)S(1)} %add_convert_fusion), channel_id=1, source_target_pairs={{0,1},{1,0},{2,3},{3,2},{4,5},{5,4},{6,7},{7,6},{8,9},{9,8},{10,11... | collective-permute-start | bytes 110600 | tf_op jit(solution)/shard_map/ppermute | solution.py:39
